TPU v7x, 128 devices: a whole 4x4x4 slice. The times are simulated.
128 devices in a mesh: lat: 8 (over x_lo, y), lon: 16 (over z, x_hi, core).
Axes of the slice: x: 4 (x_hi: 2, x_lo: 2; x = x_hi * 2 + x_lo), y: 4, z: 4, core: 2. Of those that a mesh axis runs over, the one named last changes fastest.
Arguments:
- grad_rows: bfloat16 [131072, 128], P(('lat', 'lon')), may hold values from -6 to 6
- owner: int32 [131072, 1], P(('lat', 'lon')), may hold values from 0 to 127; in each aligned block of 1024 rows (0 to 1023, 1024 to 2047, ...) at most 16 rows name the same one
- lat_offset: int32 [131072], P(('lat', 'lon')), may hold values from 0 to 63
- lon_offset: int32 [131072], P(('lat', 'lon')), may hold values from 0 to 127
- position: bfloat16 [131072, 2], P(('lat', 'lon')), may hold values from 0 to 1
- live_count: int32 [128], P(('lat', 'lon')), may hold values from 512 to 1024
- features: bfloat16 [512, 2048, 128], P('lat', 'lon'), may hold values from -6 to 6
- conv_weight: bfloat16 [3, 3, 128, 128], replicated, may hold values from -0.1875 to 0.1875
Outputs:
- input_grad: bfloat16 [512, 2048, 128], P('lat', 'lon')
- weight_grad: float32 [3, 3, 128, 128], replicated
Inputs may be any that keep to these rules, and one draw needn't show every extreme that they name: `owner`: among the 1024 rows of one device no tile is named more than 16 times, a bound that some block reaches. `live_count`: entry k counts the real rows among the rows of device k, which come first.
All inputs are finite; a program needn't handle non-finite values.
Results may differ from a plain program's by a relative error of at most 0.012.
Values may be sent and summed in bfloat16 or wider, within the bound.
No kernel may reach another device: no remote copies, remote signals or barrier semaphores. Data moves between devices by JAX's collectives and lax.ppermute only.
A program may use at most 128 MiB of HBM per device.

v0:
```python
import math
import jax
import jax.numpy as jnp
from jax import lax
from jax.sharding import PartitionSpec as P

rbf_scale = 1.5


def padded_2(cells, sides, width, closed):
    for axis, dim in sides:
        count = lax.axis_size(axis)
        ends = count if closed else count - 1
        head = lax.slice_in_dim(cells, 0, width, axis=dim)
        tail = lax.slice_in_dim(cells, cells.shape[dim] - width, cells.shape[dim], axis=dim)
        cells = jnp.concatenate(
            [
                lax.ppermute(tail, axis, [(i, (i + 1) % count) for i in range(ends)]),
                cells,
                lax.ppermute(head, axis, [((i + 1) % count, i) for i in range(ends)]),
            ],
            axis=dim,
        )
    return cells


def cut_along(value, dim, count):
    before, after = (value.shape[:dim], value.shape[dim + 1 :])
    return jnp.moveaxis(value.reshape(*before, count, -1, *after), dim, 0)


def in_order(parts, dim):
    shape = list(parts.shape[1:])
    shape[dim] *= parts.shape[0]
    return jnp.moveaxis(parts, 0, dim).reshape(shape)


def one_exchange(value, axis, axes, splits, concats):
    sizes = [lax.axis_size(a) for a in axes]
    parts = cut_along(value, splits[0], sizes[0])
    parts = jnp.moveaxis(cut_along(parts, splits[1] + 1, sizes[1]), 0, 1)
    inside = parts.shape[2:]
    parts = parts.reshape(-1, *inside)
    parts = lax.all_to_all(parts, axis, split_axis=0, concat_axis=0, tiled=True)
    parts = in_order(parts.reshape(*sizes, *inside), concats[0] + 1)
    return in_order(parts, concats[1])


def profile(frac):
    tap_index = jnp.arange(8).astype(frac.dtype)
    return jnp.exp(
        -jnp.square(tap_index[None, :] - 3.0 - frac[:, None]) / (2.0 * rbf_scale * rbf_scale)
    )


def clear_rim(padded):
    lat_index = lax.axis_index("lat")
    lat_count = lax.axis_size("lat")
    row_line = jnp.arange(padded.shape[0], dtype=jnp.int32)
    masked = (row_line == 0) & (lat_index == 0) | (row_line == padded.shape[0] - 1) & (
        lat_index == lat_count - 1
    )
    return jnp.where(masked[:, None, None], jnp.zeros_like(padded), padded)


def tap_matrix(offsets, weights, extent):
    tap_ints = jnp.arange(8, dtype=jnp.int32)
    cells = offsets[:, None] + tap_ints[None, :] + 1
    line = jnp.arange(extent, dtype=jnp.int32)
    picked = jnp.where(
        cells[:, :, None] == line[None, None, :], weights.astype(jnp.float32)[:, :, None], 0.0
    )
    return jnp.sum(picked, axis=1).astype(jnp.bfloat16)


def shards(grad_rows, owner, lat_offset, lon_offset, position, live_count, features, conv_weight):
    lat_total = lax.axis_size("lat")
    lon_total = lax.axis_size("lon")
    device_total = lat_total * lon_total
    row_total = grad_rows.shape[0]
    channels = grad_rows.shape[1]
    tile_lat = features.shape[0]
    tile_lon = features.shape[1]
    capacity = max(2, 2 * row_total // device_total)
    input_padded = clear_rim(padded_2(features, (("lat", 0), ("lon", 1)), 1, True))
    owner_tile = owner[:, 0]
    is_live = jnp.arange(row_total, dtype=jnp.int32) < live_count[0]
    matches = (
        (owner_tile[:, None] == jnp.arange(device_total, dtype=jnp.int32)[None, :])
        & is_live[:, None]
    ).astype(jnp.int32)
    earlier = jnp.cumsum(matches, axis=0) - matches
    slot_rank = jnp.sum(earlier * matches, axis=1)
    slot_index = jnp.where(is_live, owner_tile * capacity + slot_rank, device_total * capacity)
    outgoing = (
        jnp.zeros((device_total * capacity, channels), jnp.bfloat16)
        .at[slot_index]
        .set(grad_rows, mode="drop")
    )
    geometry = jnp.stack(
        [
            position[:, 0],
            position[:, 1],
            lat_offset.astype(jnp.bfloat16),
            lon_offset.astype(jnp.bfloat16),
        ],
        axis=1,
    )
    place_out = (
        jnp.zeros((device_total * capacity, 4), jnp.bfloat16)
        .at[slot_index]
        .set(geometry, mode="drop")
    )
    incoming, place_in = (
        one_exchange(
            outgoing.reshape(lat_total, lon_total, capacity, channels),
            ("lat", "lon"),
            ("lat", "lon"),
            (0, 1),
            (0, 1),
        ),
        one_exchange(
            place_out.reshape(lat_total, lon_total, capacity, 4),
            ("lat", "lon"),
            ("lat", "lon"),
            (0, 1),
            (0, 1),
        ),
    )
    incoming = incoming.reshape(-1, channels)
    place_in = place_in.reshape(-1, 4).astype(jnp.float32)
    padded_lat = tile_lat + 8
    padded_lon = tile_lon + 8
    slot_total = incoming.shape[0]
    block_rows = math.gcd(slot_total, 256)

    def accumulate(canvas, payload):
        rows_blk, place_blk = payload
        lat_weight = profile(place_blk[:, 0]).astype(jnp.bfloat16)
        lon_weight = profile(place_blk[:, 1]).astype(jnp.bfloat16)
        lat_matrix = tap_matrix(place_blk[:, 2].astype(jnp.int32), lat_weight, padded_lat)
        lon_matrix = tap_matrix(place_blk[:, 3].astype(jnp.int32), lon_weight, padded_lon)
        spread = (lon_matrix[:, :, None] * rows_blk[:, None, :]).reshape(
            rows_blk.shape[0], padded_lon * channels
        )
        canvas = canvas + lax.dot_general(
            lat_matrix, spread, (((0,), (0,)), ((), ())), preferred_element_type=jnp.float32
        )
        return (canvas, None)

    canvas, _ = lax.scan(
        accumulate,
        jnp.zeros((padded_lat, padded_lon * channels), jnp.float32),
        (incoming.reshape(-1, block_rows, channels), place_in.reshape(-1, block_rows, 4)),
    )
    canvas = canvas.reshape(padded_lat, padded_lon, channels)
    edge_rows = jnp.concatenate([canvas[:5], canvas[-5:]], axis=0)
    edge_rows = padded_2(edge_rows.astype(jnp.bfloat16), (("lat", 0),), 5, False).astype(
        edge_rows.dtype
    )
    inner = canvas[4:-4]
    inner = inner.at[:4].add(edge_rows[1:5]).at[-4:].add(edge_rows[15:19])
    rim_top = edge_rows[0] + canvas[3]
    rim_bottom = canvas[-4] + edge_rows[19]
    tall = jnp.concatenate([rim_top[None], inner, rim_bottom[None]], axis=0)
    side_cols = jnp.concatenate([tall[:, :5], tall[:, -5:]], axis=1)
    side_cols = padded_2(side_cols.astype(jnp.bfloat16), (("lon", 1),), 5, True).astype(
        side_cols.dtype
    )
    middle = tall[:, 4:-4]
    middle = middle.at[:, :4].add(side_cols[:, 1:5]).at[:, -4:].add(side_cols[:, 15:19])
    rim_left = side_cols[:, 0] + tall[:, 3]
    rim_right = tall[:, -4] + side_cols[:, 19]
    whole = jnp.concatenate([rim_left[:, None], middle, rim_right[:, None]], axis=1)
    grid_padded = clear_rim(whole.astype(jnp.bfloat16))
    grid_grad = grid_padded[1:-1, 1:-1]
    flat_grad = grid_grad.reshape(-1, channels)
    input_grad = jnp.zeros((tile_lat * tile_lon, channels), jnp.float32)
    weight_parts = []
    for a in range(3):
        for b in range(3):
            shifted = grid_padded[2 - a : 2 - a + tile_lat, 2 - b : 2 - b + tile_lon].reshape(
                -1, channels
            )
            input_grad = input_grad + lax.dot_general(
                shifted,
                conv_weight[a, b],
                (((1,), (1,)), ((), ())),
                preferred_element_type=jnp.float32,
            )
            window = input_padded[a : a + tile_lat, b : b + tile_lon].reshape(-1, channels)
            weight_parts.append(
                lax.dot_general(
                    window, flat_grad, (((0,), (0,)), ((), ())), preferred_element_type=jnp.float32
                )
            )
    weight_grad = lax.psum(
        jnp.stack(weight_parts).reshape(3, 3, channels, channels), ("lat", "lon")
    )
    return (input_grad.reshape(tile_lat, tile_lon, channels).astype(jnp.bfloat16), weight_grad)


def solution(mesh):
    placed = (
        P(("lat", "lon"), None),
        P(("lat", "lon"), None),
        P(("lat", "lon")),
        P(("lat", "lon")),
        P(("lat", "lon"), None),
        P(("lat", "lon")),
        P("lat", "lon", None),
        P(),
    )
    return jax.shard_map(
        shards, mesh=mesh, in_specs=placed, out_specs=(P("lat", "lon", None), P()), check_vma=False
    )
```

profile of v0, /device:TPU:1, one launch (start us, length us, event | category | flops | bytes accessed | tf_op | source)
XLA Modules:
  0.0 357.4 jit_solution(9674923736870181824)
XLA Ops:
  8.0 4.5 %collective-permute-start.5 = (bf16[1,128,128]{2,1,0:T(8,128)(2,1)S(1)}, bf16[1,128,128]{2,1,0:T(8,128)(2,1)S(1)}, u32[]{:S(2)}, u32[]{:S(2)}) collective-permute-start(bf16[1,128,128]{2,1,0:T(8,128)(2,1)S(1)} %get-tuple-element.168), channel_id=1, source_target_pairs={{16,0},{32,16},{48,32},{64,48},{80,64},{96,80},{112,96},{0,112},{1... | collective-permute-start | bytes 98312 | tf_op jit(solution)/shard_map/ppermute | solution.py:20
  22.2 11.0 %all-to-all-start = ((bf16[128,1,1,16,4]{3,4,2,1,0:T(4,128)(2,1)}), bf16[128,1,1,16,4]{3,4,2,1,0:T(4,128)(2,1)S(1)}, u32[]{:S(2)}, u32[]{:S(2)}) async-start(bf16[128,1,1,16,4]{3,4,2,1,0:T(4,128)(2,1)} %copy.87), calls=%async_computation | async-start | bytes 262144 | tf_op jit(solution)/shard_map/all_to_all | solution.py:44
  33.2 4.3 %scatter_custom_fusion.1 = bf16[2048,128]{1,0:T(8,128)(2,1)} fusion(s32[1024]{0:T(1024)S(1)} %bitcast.226, bf16[1024,128]{1,0:T(8,128)(2,1)} %param.18, bf16[]{:T(256)} %constant.168.clone.1), kind=kCustom, calls=%fused_computation.87 | custom fusion | bytes 524800 | tf_op jit(solution)/shard_map/scatter | solution.py:98
  37.5 5.6 %all-to-all-done = bf16[128,1,1,16,4]{3,4,2,1,0:T(4,128)(2,1)S(1)} async-done(((bf16[128,1,1,16,4]{3,4,2,1,0:T(4,128)(2,1)}), bf16[128,1,1,16,4]{3,4,2,1,0:T(4,128)(2,1)S(1)}, u32[]{:S(2)}, u32[]{:S(2)}) %all-to-all-start) | async-done | bytes 16416 | tf_op jit(solution)/shard_map/all_to_all | solution.py:44
  43.1 4.2 %all-to-all-start.1 = ((bf16[128,1,1,16,128]{4,3,2,1,0:T(8,128)(2,1)}), bf16[128,1,1,16,128]{4,3,2,1,0:T(8,128)(2,1)S(1)}, u32[]{:S(2)}, u32[]{:S(2)}) async-start(bf16[128,1,1,16,128]{4,3,2,1,0:T(8,128)(2,1)} %bitcast.13), calls=%async_computation.1 | async-start | bytes 1048576 | tf_op jit(solution)/shard_map/all_to_all | solution.py:44
  53.2 8.2 %all-to-all-done.1 = bf16[128,1,1,16,128]{4,3,2,1,0:T(8,128)(2,1)S(1)} async-done(((bf16[128,1,1,16,128]{4,3,2,1,0:T(8,128)(2,1)}), bf16[128,1,1,16,128]{4,3,2,1,0:T(8,128)(2,1)S(1)}, u32[]{:S(2)}, u32[]{:S(2)}) %all-to-all-start.1) | async-done | bytes 524320 | tf_op jit(solution)/shard_map/all_to_all | solution.py:44
  61.4 91.8 %while.17 = (s32[]{:T(128)}, f32[72,17408]{1,0:T(8,128)}, f32[8,256,4]{1,2,0:T(4,128)S(1)}, bf16[8,256,128]{2,1,0:T(8,128)(2,1)S(1)}, s32[]{:T(128)}, /*index=5*/s32[]{:T(128)}) while((s32[]{:T(128)}, f32[72,17408]{1,0:T(8,128)}, f32[8,256,4]{1,2,0:T(4,128)S(1)}, bf16[8,256,128]{2,1,0:T(8,128)(2,1)S(1)}, s32[]{:T(128)}, ...), condition=%wide.region_8.9_spmd.clone, body=%wide.region_5.8_spmd.clone.sunk | while | flops 649949696 | bytes 63582440 | solution.py:151
  61.9 5.2 %broadcast_multiply_fusion.2 = bf16[256,136,128]{2,1,0:T(8,128)(2,1)S(1)} fusion(bf16[256,128]{1,0:T(8,128)(2,1)S(1)} %dynamic-slice_bitcast_fusion.4, bf16[256,136]{1,0:T(8,128)(2,1)S(1)} %copy.129), kind=kLoop, calls=%fused_computation.5.clone.1 | loop fusion | flops 4456448 | bytes 9048064 | tf_op jit(solution)/shard_map/while/body/eval_jaxpr/mul | solution.py:143
  73.4 5.2 %broadcast_multiply_fusion.2 = bf16[256,136,128]{2,1,0:T(8,128)(2,1)S(1)} fusion(bf16[256,128]{1,0:T(8,128)(2,1)S(1)} %dynamic-slice_bitcast_fusion.4, bf16[256,136]{1,0:T(8,128)(2,1)S(1)} %copy.129), kind=kLoop, calls=%fused_computation.5.clone.1 | loop fusion | flops 4456448 | bytes 9048064 | tf_op jit(solution)/shard_map/while/body/eval_jaxpr/mul | solution.py:143
  84.8 5.2 %broadcast_multiply_fusion.2 = bf16[256,136,128]{2,1,0:T(8,128)(2,1)S(1)} fusion(bf16[256,128]{1,0:T(8,128)(2,1)S(1)} %dynamic-slice_bitcast_fusion.4, bf16[256,136]{1,0:T(8,128)(2,1)S(1)} %copy.129), kind=kLoop, calls=%fused_computation.5.clone.1 | loop fusion | flops 4456448 | bytes 9048064 | tf_op jit(solution)/shard_map/while/body/eval_jaxpr/mul | solution.py:143
  90.1 3.6 convolution_add_fusion.10
  96.3 5.2 %broadcast_multiply_fusion.2 = bf16[256,136,128]{2,1,0:T(8,128)(2,1)S(1)} fusion(bf16[256,128]{1,0:T(8,128)(2,1)S(1)} %dynamic-slice_bitcast_fusion.4, bf16[256,136]{1,0:T(8,128)(2,1)S(1)} %copy.129), kind=kLoop, calls=%fused_computation.5.clone.1 | loop fusion | flops 4456448 | bytes 9048064 | tf_op jit(solution)/shard_map/while/body/eval_jaxpr/mul | solution.py:143
  101.5 3.6 convolution_add_fusion.10
  107.8 5.2 %broadcast_multiply_fusion.2 = bf16[256,136,128]{2,1,0:T(8,128)(2,1)S(1)} fusion(bf16[256,128]{1,0:T(8,128)(2,1)S(1)} %dynamic-slice_bitcast_fusion.4, bf16[256,136]{1,0:T(8,128)(2,1)S(1)} %copy.129), kind=kLoop, calls=%fused_computation.5.clone.1 | loop fusion | flops 4456448 | bytes 9048064 | tf_op jit(solution)/shard_map/while/body/eval_jaxpr/mul | solution.py:143
  113.0 3.6 convolution_add_fusion.10
  119.3 5.2 %broadcast_multiply_fusion.2 = bf16[256,136,128]{2,1,0:T(8,128)(2,1)S(1)} fusion(bf16[256,128]{1,0:T(8,128)(2,1)S(1)} %dynamic-slice_bitcast_fusion.4, bf16[256,136]{1,0:T(8,128)(2,1)S(1)} %copy.129), kind=kLoop, calls=%fused_computation.5.clone.1 | loop fusion | flops 4456448 | bytes 9048064 | tf_op jit(solution)/shard_map/while/body/eval_jaxpr/mul | solution.py:143
  124.5 3.6 convolution_add_fusion.10
  130.8 5.2 %broadcast_multiply_fusion.2 = bf16[256,136,128]{2,1,0:T(8,128)(2,1)S(1)} fusion(bf16[256,128]{1,0:T(8,128)(2,1)S(1)} %dynamic-slice_bitcast_fusion.4, bf16[256,136]{1,0:T(8,128)(2,1)S(1)} %copy.129), kind=kLoop, calls=%fused_computation.5.clone.1 | loop fusion | flops 4456448 | bytes 9048064 | tf_op jit(solution)/shard_map/while/body/eval_jaxpr/mul | solution.py:143
  136.0 3.6 convolution_add_fusion.10
  142.2 5.2 %broadcast_multiply_fusion.2 = bf16[256,136,128]{2,1,0:T(8,128)(2,1)S(1)} fusion(bf16[256,128]{1,0:T(8,128)(2,1)S(1)} %dynamic-slice_bitcast_fusion.4, bf16[256,136]{1,0:T(8,128)(2,1)S(1)} %copy.129), kind=kLoop, calls=%fused_computation.5.clone.1 | loop fusion | flops 4456448 | bytes 9048064 | tf_op jit(solution)/shard_map/while/body/eval_jaxpr/mul | solution.py:143
  161.1 4.0 %collective-permute-start = (bf16[5,136,128]{2,1,0:T(8,128)(2,1)S(1)}, bf16[5,136,128]{2,1,0:T(8,128)(2,1)S(1)}, u32[]{:S(2)}, u32[]{:S(2)}) collective-permute-start(bf16[5,136,128]{2,1,0:T(8,128)(2,1)S(1)} %bitcast.203), channel_id=1, source_target_pairs={{0,16},{16,32},{32,48},{48,64},{64,80},{80,96},{96,112},{1,17},{17... | collective-permute-start | bytes 522248 | tf_op jit(solution)/shard_map/ppermute | solution.py:18
  172.8 4.2 %collective-permute-done.3 = bf16[66,5,128]{2,1,0:T(8,128)(2,1)S(1)} collective-permute-done((bf16[66,5,128]{2,1,0:T(8,128)(2,1)S(1)}, bf16[66,5,128]{2,1,0:T(8,128)(2,1)S(1)}, u32[]{:S(2)}, u32[]{:S(2)}) %collective-permute-start.3) | collective-permute-done | bytes 84512 | tf_op jit(solution)/shard_map/ppermute | solution.py:20
  181.1 7.0 %fusion.129 = (bf16[64,128,128]{2,1,0:T(8,128)(2,1)}, bf16[64,128,128]{2,1,0:T(8,128)(2,1)S(1)}, bf16[64,128,128]{2,1,0:T(8,128)(2,1)}, bf16[64,128,128]{2,1,0:T...) fusion(bf16[66,130,128]{2,1,0:T(8,128)(2,1)S(1)} %get-tuple-ele, ...), kind=kLoop, calls=%fused_computation.153 | loop fusion | bytes 37748736 | tf_op jit(solution)/shard_map/slice | solution.py:182
  214.3 134.3 %all-reduce.2.cloned.1.call-done = f32[3,3,128,128]{3,2,1,0:T(8,128)} async-done(((f32[3,3,128,128]{3,2,1,0:T(8,128)}), f32[3,3,128,128]{3,2,1,0:T(8,128)}) %all-reduce.2.cloned.1.call-update) | async-done | bytes 589840 | tf_op jit(solution)/shard_map/psum | solution.py:197
  (245 shorter events, 94.9 us)
Async XLA Ops:
  7.2 9.6 %copy-start.11 = (s32[1024,1]{0,1:T(1,128)S(1)}, s32[1024,1]{0,1:T(1,128)}, u32[]{:S(2)}) copy-start(s32[1024,1]{0,1:T(1,128)} %param.19) | copy-start | bytes 12292
  8.0 41.9 %collective-permute-start.5 = (bf16[1,128,128]{2,1,0:T(8,128)(2,1)S(1)}, bf16[1,128,128]{2,1,0:T(8,128)(2,1)S(1)}, u32[]{:S(2)}, u32[]{:S(2)}) collective-permute-start(bf16[1,128,128]{2,1,0:T(8,128)(2,1)S(1)} %get-tuple-element.168), channel_id=1, source_target_pairs={{16,0},{32,16},{48,32},{64,48},{80,64},{96,80},{112,96},{0,112},{1... | collective-permute-start | bytes 98312 | tf_op jit(solution)/shard_map/ppermute | solution.py:20
  12.5 35.4 %collective-permute-start.4 = (bf16[1,128,128]{2,1,0:T(8,128)(2,1)S(1)}, bf16[1,128,128]{2,1,0:T(8,128)(2,1)S(1)}, u32[]{:S(2)}, u32[]{:S(2)}) collective-permute-start(bf16[1,128,128]{2,1,0:T(8,128)(2,1)S(1)} %get-tuple-element.169), channel_id=1, source_target_pairs={{0,16},{16,32},{32,48},{48,64},{64,80},{80,96},{96,112},{112,0},{1... | collective-permute-start | bytes 98312 | tf_op jit(solution)/shard_map/ppermute | solution.py:18
  22.2 20.9 %all-to-all-start = ((bf16[128,1,1,16,4]{3,4,2,1,0:T(4,128)(2,1)}), bf16[128,1,1,16,4]{3,4,2,1,0:T(4,128)(2,1)S(1)}, u32[]{:S(2)}, u32[]{:S(2)}) async-start(bf16[128,1,1,16,4]{3,4,2,1,0:T(4,128)(2,1)} %copy.87), calls=%async_computation | async-start | bytes 262144 | tf_op jit(solution)/shard_map/all_to_all | solution.py:44
  43.1 18.3 %all-to-all-start.1 = ((bf16[128,1,1,16,128]{4,3,2,1,0:T(8,128)(2,1)}), bf16[128,1,1,16,128]{4,3,2,1,0:T(8,128)(2,1)S(1)}, u32[]{:S(2)}, u32[]{:S(2)}) async-start(bf16[128,1,1,16,128]{4,3,2,1,0:T(8,128)(2,1)} %bitcast.13), calls=%async_computation.1 | async-start | bytes 1048576 | tf_op jit(solution)/shard_map/all_to_all | solution.py:44
  47.3 301.3 %all-reduce.2.cloned.1.call-start = ((), (), s32[]{:S(2)}) async-start(), calls=%async_computation.2 | async-start | bytes 1179648 | tf_op jit(solution)/shard_map/psum | solution.py:197
  50.0 128.0 %collective-permute-start.6 = (bf16[66,1,128]{2,1,0:T(2,128)(2,1)S(1)}, bf16[66,1,128]{2,1,0:T(2,128)(2,1)S(1)}, u32[]{:S(2)}, u32[]{:S(2)}) collective-permute-start(bf16[66,1,128]{2,1,0:T(2,128)(2,1)S(1)} %get-tuple-element.166), channel_id=1, source_target_pairs={{0,1},{1,2},{2,3},{3,4},{4,5},{5,6},{6,7},{7,8},{8,9},{9,10},{10,1... | collective-permute-start | bytes 50696 | tf_op jit(solution)/shard_map/ppermute | solution.py:18
  53.2 124.8 %collective-permute-start.7 = (bf16[66,1,128]{2,1,0:T(2,128)(2,1)S(1)}, bf16[66,1,128]{2,1,0:T(2,128)(2,1)S(1)}, u32[]{:S(2)}, u32[]{:S(2)}) collective-permute-start(bf16[66,1,128]{2,1,0:T(2,128)(2,1)S(1)} %get-tuple-element.167), channel_id=1, source_target_pairs={{1,0},{2,1},{3,2},{4,3},{5,4},{6,5},{7,6},{8,7},{9,8},{10,9},{11,1... | collective-permute-start | bytes 50696 | tf_op jit(solution)/shard_map/ppermute | solution.py:20
  61.8 5.2 %slice-start = ((s8[5013504]{0:T(1024)(128)(4,1)}), s8[4194304]{0:T(1024)(128)(4,1)S(1)}, s32[]{:S(2)}) async-start(s8[5013504]{0:T(1024)(128)(4,1)} %bitcast.191), calls=%async_computation.3 | async-start | bytes 8388608 | tf_op jit(solution)/shard_map/while
  61.9 5.2 %slice-start.1 = ((s8[5013504]{0:T(1024)(128)(4,1)}), s8[819200]{0:T(1024)(128)(4,1)S(1)}, s32[]{:S(2)}) async-start(s8[5013504]{0:T(1024)(128)(4,1)} %bitcast.191), calls=%async_computation.4 | async-start | bytes 1638400 | tf_op jit(solution)/shard_map/while
  73.3 5.2 %slice-start = ((s8[5013504]{0:T(1024)(128)(4,1)}), s8[4194304]{0:T(1024)(128)(4,1)S(1)}, s32[]{:S(2)}) async-start(s8[5013504]{0:T(1024)(128)(4,1)} %bitcast.191), calls=%async_computation.3 | async-start | bytes 8388608 | tf_op jit(solution)/shard_map/while
  73.4 5.2 %slice-start.1 = ((s8[5013504]{0:T(1024)(128)(4,1)}), s8[819200]{0:T(1024)(128)(4,1)S(1)}, s32[]{:S(2)}) async-start(s8[5013504]{0:T(1024)(128)(4,1)} %bitcast.191), calls=%async_computation.4 | async-start | bytes 1638400 | tf_op jit(solution)/shard_map/while
  84.8 5.2 %slice-start = ((s8[5013504]{0:T(1024)(128)(4,1)}), s8[4194304]{0:T(1024)(128)(4,1)S(1)}, s32[]{:S(2)}) async-start(s8[5013504]{0:T(1024)(128)(4,1)} %bitcast.191), calls=%async_computation.3 | async-start | bytes 8388608 | tf_op jit(solution)/shard_map/while
  84.8 5.2 %slice-start.1 = ((s8[5013504]{0:T(1024)(128)(4,1)}), s8[819200]{0:T(1024)(128)(4,1)S(1)}, s32[]{:S(2)}) async-start(s8[5013504]{0:T(1024)(128)(4,1)} %bitcast.191), calls=%async_computation.4 | async-start | bytes 1638400 | tf_op jit(solution)/shard_map/while
  96.3 5.2 %slice-start = ((s8[5013504]{0:T(1024)(128)(4,1)}), s8[4194304]{0:T(1024)(128)(4,1)S(1)}, s32[]{:S(2)}) async-start(s8[5013504]{0:T(1024)(128)(4,1)} %bitcast.191), calls=%async_computation.3 | async-start | bytes 8388608 | tf_op jit(solution)/shard_map/while
  107.8 5.2 %slice-start = ((s8[5013504]{0:T(1024)(128)(4,1)}), s8[4194304]{0:T(1024)(128)(4,1)S(1)}, s32[]{:S(2)}) async-start(s8[5013504]{0:T(1024)(128)(4,1)} %bitcast.191), calls=%async_computation.3 | async-start | bytes 8388608 | tf_op jit(solution)/shard_map/while
  119.2 5.2 %slice-start = ((s8[5013504]{0:T(1024)(128)(4,1)}), s8[4194304]{0:T(1024)(128)(4,1)S(1)}, s32[]{:S(2)}) async-start(s8[5013504]{0:T(1024)(128)(4,1)} %bitcast.191), calls=%async_computation.3 | async-start | bytes 8388608 | tf_op jit(solution)/shard_map/while
  119.3 5.2 %slice-start.1 = ((s8[5013504]{0:T(1024)(128)(4,1)}), s8[819200]{0:T(1024)(128)(4,1)S(1)}, s32[]{:S(2)}) async-start(s8[5013504]{0:T(1024)(128)(4,1)} %bitcast.191), calls=%async_computation.4 | async-start | bytes 1638400 | tf_op jit(solution)/shard_map/while
  130.7 5.2 %slice-start = ((s8[5013504]{0:T(1024)(128)(4,1)}), s8[4194304]{0:T(1024)(128)(4,1)S(1)}, s32[]{:S(2)}) async-start(s8[5013504]{0:T(1024)(128)(4,1)} %bitcast.191), calls=%async_computation.3 | async-start | bytes 8388608 | tf_op jit(solution)/shard_map/while
  142.2 5.2 %slice-start = ((s8[5013504]{0:T(1024)(128)(4,1)}), s8[4194304]{0:T(1024)(128)(4,1)S(1)}, s32[]{:S(2)}) async-start(s8[5013504]{0:T(1024)(128)(4,1)} %bitcast.191), calls=%async_computation.3 | async-start | bytes 8388608 | tf_op jit(solution)/shard_map/while
  159.8 7.7 %collective-permute-start.1 = (bf16[5,136,128]{2,1,0:T(8,128)(2,1)S(1)}, bf16[5,136,128]{2,1,0:T(8,128)(2,1)S(1)}, u32[]{:S(2)}, u32[]{:S(2)}) collective-permute-start(bf16[5,136,128]{2,1,0:T(8,128)(2,1)S(1)} %bitcast.207), channel_id=1, source_target_pairs={{16,0},{32,16},{48,32},{64,48},{80,64},{96,80},{112,96},{17,1},{33... | collective-permute-start | bytes 522248 | tf_op jit(solution)/shard_map/ppermute | solution.py:20
  161.1 7.2 %collective-permute-start = (bf16[5,136,128]{2,1,0:T(8,128)(2,1)S(1)}, bf16[5,136,128]{2,1,0:T(8,128)(2,1)S(1)}, u32[]{:S(2)}, u32[]{:S(2)}) collective-permute-start(bf16[5,136,128]{2,1,0:T(8,128)(2,1)S(1)} %bitcast.203), channel_id=1, source_target_pairs={{0,16},{16,32},{32,48},{48,64},{64,80},{80,96},{96,112},{1,17},{17... | collective-permute-start | bytes 522248 | tf_op jit(solution)/shard_map/ppermute | solution.py:18
  168.8 3.9 %collective-permute-start.2 = (bf16[66,5,128]{2,1,0:T(8,128)(2,1)S(1)}, bf16[66,5,128]{2,1,0:T(8,128)(2,1)S(1)}, u32[]{:S(2)}, u32[]{:S(2)}) collective-permute-start(bf16[66,5,128]{2,1,0:T(8,128)(2,1)S(1)} %get-tuple-element.164), channel_id=1, source_target_pairs={{0,1},{1,2},{2,3},{3,4},{4,5},{5,6},{6,7},{7,8},{8,9},{9,10},{10,1... | collective-permute-start | bytes 253448 | tf_op jit(solution)/shard_map/ppermute | solution.py:18
  170.8 6.2 %collective-permute-start.3 = (bf16[66,5,128]{2,1,0:T(8,128)(2,1)S(1)}, bf16[66,5,128]{2,1,0:T(8,128)(2,1)S(1)}, u32[]{:S(2)}, u32[]{:S(2)}) collective-permute-start(bf16[66,5,128]{2,1,0:T(8,128)(2,1)S(1)} %get-tuple-element.165), channel_id=1, source_target_pairs={{1,0},{2,1},{3,2},{4,3},{5,4},{6,5},{7,6},{8,7},{9,8},{10,9},{11,1... | collective-permute-start | bytes 253448 | tf_op jit(solution)/shard_map/ppermute | solution.py:20
  (22 other events, 57.7 us)
Sparse Core Ops, SparseCore 0:
  199.6 148.9 all-reduce.1
where the time goes:
time: 358 us; the launch traced here: 357 us
  waiting for transfers between devices  157 us (44%)
  other arithmetic  54.3 us (15%)
  local copies, waits for them, and re-layouts  51.6 us (14%)
  matrix products  48.7 us (14%)
  starting transfers between devices  30.1 us (8%)
  between operations  15.2 us (4%)
    psum x1, waiting for transfers between devices, shards(): lax.psum(jnp.stack(weight_parts).reshape(3, 3, channels, channels), ('lat...  134 us
    mul x8, other arithmetic, accumulate(): lon_matrix[:, :, None] * rows_blk[:, None, :]  41.4 us
    dot_general x8, matrix products, accumulate(): lax.dot_general(lat_matrix, spread, (((0,), (0,)), ((), ())), preferred_e...  28.5 us
    while x48, local copies, waits for them, and re-layouts  17.9 us
    all_to_all x2, starting transfers between devices, one_exchange(): parts = lax.all_to_all(parts, axis, split_axis=0, concat_axis=0, tiled=True)  15.1 us
    all_to_all x2, waiting for transfers between devices, one_exchange(): parts = lax.all_to_all(parts, axis, split_axis=0, concat_axis=0, tiled=True)  13.8 us
    unnamed x33, local copies, waits for them, and re-layouts  12.4 us
    dot_general x9, matrix products, shards(): lax.dot_general(window, flat_grad, (((0,), (0,)), ((), ())), preferred_el...  10.5 us
  transfers between devices with their start and end apart: 11, of which 7 were waited for; matrix products, arithmetic and copies ran while one was open for 30% of the time, Pallas kernels for 0%

commit v1 on v0

--- a/solution.py
+++ b/solution.py
@@ -194,9 +194,8 @@
                     window, flat_grad, (((0,), (0,)), ((), ())), preferred_element_type=jnp.float32
                 )
             )
-    weight_grad = lax.psum(
-        jnp.stack(weight_parts).reshape(3, 3, channels, channels), ("lat", "lon")
-    )
+    partial = lax.psum(jnp.stack(weight_parts).reshape(3, 3, channels, channels), "lat")
+    weight_grad = lax.psum(partial, "lon")
     return (input_grad.reshape(tile_lat, tile_lon, channels).astype(jnp.bfloat16), weight_grad)
 
 

time: 358 us -> 428 us (1.20)
  waiting for transfers between devices: 157 us -> 221 us
    psum x1 -> x2, waiting for transfers between devices: 134 us -> 198 us  [the longest x1 138 us: shards(): weight_grad = lax.psum(partial, 'lon')]
  transfers between devices with their start and end apart: 11 -> 12, of which waited for: 7 -> 8; matrix products, arithmetic and copies ran while one was open for 30% -> 26% of each run, Pallas kernels for 0% -> 0%
where the time goes in v1:
time: 428 us; the launch traced here: 425 us
  waiting for transfers between devices  221 us (52%)
  other arithmetic  54.3 us (13%)
  matrix products  52.7 us (12%)
  local copies, waits for them, and re-layouts  51 us (12%)
  starting transfers between devices  30.4 us (7%)
  between operations  15.2 us (4%)
    psum x1, waiting for transfers between devices, shards(): weight_grad = lax.psum(partial, 'lon')  138 us
    psum x1, waiting for transfers between devices, shards(): lax.psum(jnp.stack(weight_parts).reshape(3, 3, channels, channels), 'lat')  60.5 us
    mul x8, other arithmetic, accumulate(): lon_matrix[:, :, None] * rows_blk[:, None, :]  41.4 us
    dot_general x8, matrix products, accumulate(): lax.dot_general(lat_matrix, spread, (((0,), (0,)), ((), ())), preferred_e...  28.5 us
    while x48, local copies, waits for them, and re-layouts  17.9 us
    all_to_all x2, starting transfers between devices, one_exchange(): parts = lax.all_to_all(parts, axis, split_axis=0, concat_axis=0, tiled=True)  15.1 us
    all_to_all x2, waiting for transfers between devices, one_exchange(): parts = lax.all_to_all(parts, axis, split_axis=0, concat_axis=0, tiled=True)  13.8 us
    dot_general x9, matrix products, shards(): lax.dot_general(shifted, conv_weight[a, b], (((1,), (1,)), ((), ())), pre...  13.7 us
  transfers between devices with their start and end apart: 12, of which 8 were waited for; matrix products, arithmetic and copies ran while one was open for 26% of the time, Pallas kernels for 0%

profile of v1, /device:TPU:1, one launch (start us, length us, event | category | flops | bytes accessed | tf_op | source)
XLA Modules:
  0.0 425.0 jit_solution(77586554242475950)
XLA Ops:
  8.0 4.5 %collective-permute-start.5 = (bf16[1,128,128]{2,1,0:T(8,128)(2,1)S(1)}, bf16[1,128,128]{2,1,0:T(8,128)(2,1)S(1)}, u32[]{:S(2)}, u32[]{:S(2)}) collective-permute-start(bf16[1,128,128]{2,1,0:T(8,128)(2,1)S(1)} %get-tuple-element.168), channel_id=1, source_target_pairs={{16,0},{32,16},{48,32},{64,48},{80,64},{96,80},{112,96},{0,112},{1... | collective-permute-start | bytes 98312 | tf_op jit(solution)/shard_map/ppermute | solution.py:20
  22.2 11.0 %all-to-all-start = ((bf16[128,1,1,16,4]{3,4,2,1,0:T(4,128)(2,1)}), bf16[128,1,1,16,4]{3,4,2,1,0:T(4,128)(2,1)S(1)}, u32[]{:S(2)}, u32[]{:S(2)}) async-start(bf16[128,1,1,16,4]{3,4,2,1,0:T(4,128)(2,1)} %copy.87), calls=%async_computation | async-start | bytes 262144 | tf_op jit(solution)/shard_map/all_to_all | solution.py:44
  33.2 4.3 %scatter_custom_fusion.1 = bf16[2048,128]{1,0:T(8,128)(2,1)} fusion(s32[1024]{0:T(1024)S(1)} %bitcast.226, bf16[1024,128]{1,0:T(8,128)(2,1)} %param.18, bf16[]{:T(256)} %constant.168.clone.1), kind=kCustom, calls=%fused_computation.87 | custom fusion | bytes 524800 | tf_op jit(solution)/shard_map/scatter | solution.py:98
  37.5 5.6 %all-to-all-done = bf16[128,1,1,16,4]{3,4,2,1,0:T(4,128)(2,1)S(1)} async-done(((bf16[128,1,1,16,4]{3,4,2,1,0:T(4,128)(2,1)}), bf16[128,1,1,16,4]{3,4,2,1,0:T(4,128)(2,1)S(1)}, u32[]{:S(2)}, u32[]{:S(2)}) %all-to-all-start) | async-done | bytes 16416 | tf_op jit(solution)/shard_map/all_to_all | solution.py:44
  43.1 4.2 all-to-all-start.1
  53.2 8.2 %all-to-all-done.1 = bf16[128,1,1,16,128]{4,3,2,1,0:T(8,128)(2,1)S(1)} async-done(((bf16[128,1,1,16,128]{4,3,2,1,0:T(8,128)(2,1)}), bf16[128,1,1,16,128]{4,3,2,1,0:T(8,128)(2,1)S(1)}, u32[]{:S(2)}, u32[]{:S(2)}) %all-to-all-start.1) | async-done | bytes 524320 | tf_op jit(solution)/shard_map/all_to_all | solution.py:44
  61.4 91.8 %while.17 = (s32[]{:T(128)}, f32[72,17408]{1,0:T(8,128)}, f32[8,256,4]{1,2,0:T(4,128)S(1)}, bf16[8,256,128]{2,1,0:T(8,128)(2,1)S(1)}, s32[]{:T(128)}, /*index=5*/s32[]{:T(128)}) while((s32[]{:T(128)}, f32[72,17408]{1,0:T(8,128)}, f32[8,256,4]{1,2,0:T(4,128)S(1)}, bf16[8,256,128]{2,1,0:T(8,128)(2,1)S(1)}, s32[]{:T(128)}, ...), condition=%wide.region_8.9_spmd.clone, body=%wide.region_5.8_spmd.clone.sunk | while | flops 649949696 | bytes 63582440 | solution.py:151
  61.9 5.2 %broadcast_multiply_fusion.2 = bf16[256,136,128]{2,1,0:T(8,128)(2,1)S(1)} fusion(bf16[256,128]{1,0:T(8,128)(2,1)S(1)} %dynamic-slice_bitcast_fusion.4, bf16[256,136]{1,0:T(8,128)(2,1)S(1)} %copy.129), kind=kLoop, calls=%fused_computation.5.clone.1 | loop fusion | flops 4456448 | bytes 9048064 | tf_op jit(solution)/shard_map/while/body/eval_jaxpr/mul | solution.py:143
  73.4 5.2 %broadcast_multiply_fusion.2 = bf16[256,136,128]{2,1,0:T(8,128)(2,1)S(1)} fusion(bf16[256,128]{1,0:T(8,128)(2,1)S(1)} %dynamic-slice_bitcast_fusion.4, bf16[256,136]{1,0:T(8,128)(2,1)S(1)} %copy.129), kind=kLoop, calls=%fused_computation.5.clone.1 | loop fusion | flops 4456448 | bytes 9048064 | tf_op jit(solution)/shard_map/while/body/eval_jaxpr/mul | solution.py:143
  84.8 5.2 %broadcast_multiply_fusion.2 = bf16[256,136,128]{2,1,0:T(8,128)(2,1)S(1)} fusion(bf16[256,128]{1,0:T(8,128)(2,1)S(1)} %dynamic-slice_bitcast_fusion.4, bf16[256,136]{1,0:T(8,128)(2,1)S(1)} %copy.129), kind=kLoop, calls=%fused_computation.5.clone.1 | loop fusion | flops 4456448 | bytes 9048064 | tf_op jit(solution)/shard_map/while/body/eval_jaxpr/mul | solution.py:143
  90.1 3.6 convolution_add_fusion.10
  96.3 5.2 %broadcast_multiply_fusion.2 = bf16[256,136,128]{2,1,0:T(8,128)(2,1)S(1)} fusion(bf16[256,128]{1,0:T(8,128)(2,1)S(1)} %dynamic-slice_bitcast_fusion.4, bf16[256,136]{1,0:T(8,128)(2,1)S(1)} %copy.129), kind=kLoop, calls=%fused_computation.5.clone.1 | loop fusion | flops 4456448 | bytes 9048064 | tf_op jit(solution)/shard_map/while/body/eval_jaxpr/mul | solution.py:143
  101.5 3.6 convolution_add_fusion.10
  107.8 5.2 %broadcast_multiply_fusion.2 = bf16[256,136,128]{2,1,0:T(8,128)(2,1)S(1)} fusion(bf16[256,128]{1,0:T(8,128)(2,1)S(1)} %dynamic-slice_bitcast_fusion.4, bf16[256,136]{1,0:T(8,128)(2,1)S(1)} %copy.129), kind=kLoop, calls=%fused_computation.5.clone.1 | loop fusion | flops 4456448 | bytes 9048064 | tf_op jit(solution)/shard_map/while/body/eval_jaxpr/mul | solution.py:143
  113.0 3.6 convolution_add_fusion.10
  119.3 5.2 %broadcast_multiply_fusion.2 = bf16[256,136,128]{2,1,0:T(8,128)(2,1)S(1)} fusion(bf16[256,128]{1,0:T(8,128)(2,1)S(1)} %dynamic-slice_bitcast_fusion.4, bf16[256,136]{1,0:T(8,128)(2,1)S(1)} %copy.129), kind=kLoop, calls=%fused_computation.5.clone.1 | loop fusion | flops 4456448 | bytes 9048064 | tf_op jit(solution)/shard_map/while/body/eval_jaxpr/mul | solution.py:143
  124.5 3.6 convolution_add_fusion.10
  130.8 5.2 %broadcast_multiply_fusion.2 = bf16[256,136,128]{2,1,0:T(8,128)(2,1)S(1)} fusion(bf16[256,128]{1,0:T(8,128)(2,1)S(1)} %dynamic-slice_bitcast_fusion.4, bf16[256,136]{1,0:T(8,128)(2,1)S(1)} %copy.129), kind=kLoop, calls=%fused_computation.5.clone.1 | loop fusion | flops 4456448 | bytes 9048064 | tf_op jit(solution)/shard_map/while/body/eval_jaxpr/mul | solution.py:143
  142.2 5.2 %broadcast_multiply_fusion.2 = bf16[256,136,128]{2,1,0:T(8,128)(2,1)S(1)} fusion(bf16[256,128]{1,0:T(8,128)(2,1)S(1)} %dynamic-slice_bitcast_fusion.4, bf16[256,136]{1,0:T(8,128)(2,1)S(1)} %copy.129), kind=kLoop, calls=%fused_computation.5.clone.1 | loop fusion | flops 4456448 | bytes 9048064 | tf_op jit(solution)/shard_map/while/body/eval_jaxpr/mul | solution.py:143
  161.1 4.0 collective-permute-start
  172.8 4.2 collective-permute-done.3
  181.1 7.0 %fusion.129 = (bf16[64,128,128]{2,1,0:T(8,128)(2,1)}, bf16[64,128,128]{2,1,0:T(8,128)(2,1)S(1)}, bf16[64,128,128]{2,1,0:T(8,128)(2,1)}, bf16[64,128,128]{2,1,0:T...) fusion(bf16[66,130,128]{2,1,0:T(8,128)(2,1)S(1)} %get-tuple-ele, ...), kind=kLoop, calls=%fused_computation.153 | loop fusion | bytes 37748736 | tf_op jit(solution)/shard_map/slice | solution.py:182
  212.9 60.5 %all-reduce.3.cloned.1.call-done = f32[3,3,128,128]{3,2,1,0:T(8,128)} async-done(((f32[3,3,128,128]{3,2,1,0:T(8,128)}), f32[3,3,128,128]{3,2,1,0:T(8,128)}) %all-reduce.3.cloned.1.call-update) | async-done | bytes 589840 | tf_op jit(solution)/shard_map/psum | solution.py:197
  278.6 137.7 %all-reduce.5.cloned.1.call-done = f32[3,3,128,128]{3,2,1,0:T(8,128)} async-done(((f32[3,3,128,128]{3,2,1,0:T(8,128)}), f32[3,3,128,128]{3,2,1,0:T(8,128)}) %all-reduce.5.cloned.1.call-update) | async-done | bytes 589840 | tf_op jit(solution)/shard_map/psum | solution.py:198
  (248 shorter events, 102.1 us)
Async XLA Ops:
  7.2 9.6 %copy-start.11 = (s32[1024,1]{0,1:T(1,128)S(1)}, s32[1024,1]{0,1:T(1,128)}, u32[]{:S(2)}) copy-start(s32[1024,1]{0,1:T(1,128)} %param.19) | copy-start | bytes 12292
  8.0 41.9 %collective-permute-start.5 = (bf16[1,128,128]{2,1,0:T(8,128)(2,1)S(1)}, bf16[1,128,128]{2,1,0:T(8,128)(2,1)S(1)}, u32[]{:S(2)}, u32[]{:S(2)}) collective-permute-start(bf16[1,128,128]{2,1,0:T(8,128)(2,1)S(1)} %get-tuple-element.168), channel_id=1, source_target_pairs={{16,0},{32,16},{48,32},{64,48},{80,64},{96,80},{112,96},{0,112},{1... | collective-permute-start | bytes 98312 | tf_op jit(solution)/shard_map/ppermute | solution.py:20
  12.5 35.4 %collective-permute-start.4 = (bf16[1,128,128]{2,1,0:T(8,128)(2,1)S(1)}, bf16[1,128,128]{2,1,0:T(8,128)(2,1)S(1)}, u32[]{:S(2)}, u32[]{:S(2)}) collective-permute-start(bf16[1,128,128]{2,1,0:T(8,128)(2,1)S(1)} %get-tuple-element.169), channel_id=1, source_target_pairs={{0,16},{16,32},{32,48},{48,64},{64,80},{80,96},{96,112},{112,0},{1... | collective-permute-start | bytes 98312 | tf_op jit(solution)/shard_map/ppermute | solution.py:18
  22.2 20.9 %all-to-all-start = ((bf16[128,1,1,16,4]{3,4,2,1,0:T(4,128)(2,1)}), bf16[128,1,1,16,4]{3,4,2,1,0:T(4,128)(2,1)S(1)}, u32[]{:S(2)}, u32[]{:S(2)}) async-start(bf16[128,1,1,16,4]{3,4,2,1,0:T(4,128)(2,1)} %copy.87), calls=%async_computation | async-start | bytes 262144 | tf_op jit(solution)/shard_map/all_to_all | solution.py:44
  43.1 18.3 %all-to-all-start.1 = ((bf16[128,1,1,16,128]{4,3,2,1,0:T(8,128)(2,1)}), bf16[128,1,1,16,128]{4,3,2,1,0:T(8,128)(2,1)S(1)}, u32[]{:S(2)}, u32[]{:S(2)}) async-start(bf16[128,1,1,16,128]{4,3,2,1,0:T(8,128)(2,1)} %bitcast.13), calls=%async_computation.1 | async-start | bytes 1048576 | tf_op jit(solution)/shard_map/all_to_all | solution.py:44
  47.3 226.1 %all-reduce.3.cloned.1.call-start = ((), (), s32[]{:S(2)}) async-start(), calls=%async_computation.2 | async-start | bytes 1179648 | tf_op jit(solution)/shard_map/psum | solution.py:197
  50.0 128.0 %collective-permute-start.6 = (bf16[66,1,128]{2,1,0:T(2,128)(2,1)S(1)}, bf16[66,1,128]{2,1,0:T(2,128)(2,1)S(1)}, u32[]{:S(2)}, u32[]{:S(2)}) collective-permute-start(bf16[66,1,128]{2,1,0:T(2,128)(2,1)S(1)} %get-tuple-element.166), channel_id=1, source_target_pairs={{0,1},{1,2},{2,3},{3,4},{4,5},{5,6},{6,7},{7,8},{8,9},{9,10},{10,1... | collective-permute-start | bytes 50696 | tf_op jit(solution)/shard_map/ppermute | solution.py:18
  53.2 124.8 %collective-permute-start.7 = (bf16[66,1,128]{2,1,0:T(2,128)(2,1)S(1)}, bf16[66,1,128]{2,1,0:T(2,128)(2,1)S(1)}, u32[]{:S(2)}, u32[]{:S(2)}) collective-permute-start(bf16[66,1,128]{2,1,0:T(2,128)(2,1)S(1)} %get-tuple-element.167), channel_id=1, source_target_pairs={{1,0},{2,1},{3,2},{4,3},{5,4},{6,5},{7,6},{8,7},{9,8},{10,9},{11,1... | collective-permute-start | bytes 50696 | tf_op jit(solution)/shard_map/ppermute | solution.py:20
  61.8 5.2 %slice-start = ((s8[5013504]{0:T(1024)(128)(4,1)}), s8[4194304]{0:T(1024)(128)(4,1)S(1)}, s32[]{:S(2)}) async-start(s8[5013504]{0:T(1024)(128)(4,1)} %bitcast.191), calls=%async_computation.4 | async-start | bytes 8388608 | tf_op jit(solution)/shard_map/while
  61.9 5.2 %slice-start.1 = ((s8[5013504]{0:T(1024)(128)(4,1)}), s8[819200]{0:T(1024)(128)(4,1)S(1)}, s32[]{:S(2)}) async-start(s8[5013504]{0:T(1024)(128)(4,1)} %bitcast.191), calls=%async_computation.5 | async-start | bytes 1638400 | tf_op jit(solution)/shard_map/while
  73.3 5.2 %slice-start = ((s8[5013504]{0:T(1024)(128)(4,1)}), s8[4194304]{0:T(1024)(128)(4,1)S(1)}, s32[]{:S(2)}) async-start(s8[5013504]{0:T(1024)(128)(4,1)} %bitcast.191), calls=%async_computation.4 | async-start | bytes 8388608 | tf_op jit(solution)/shard_map/while
  73.4 5.2 %slice-start.1 = ((s8[5013504]{0:T(1024)(128)(4,1)}), s8[819200]{0:T(1024)(128)(4,1)S(1)}, s32[]{:S(2)}) async-start(s8[5013504]{0:T(1024)(128)(4,1)} %bitcast.191), calls=%async_computation.5 | async-start | bytes 1638400 | tf_op jit(solution)/shard_map/while
  84.8 5.2 %slice-start = ((s8[5013504]{0:T(1024)(128)(4,1)}), s8[4194304]{0:T(1024)(128)(4,1)S(1)}, s32[]{:S(2)}) async-start(s8[5013504]{0:T(1024)(128)(4,1)} %bitcast.191), calls=%async_computation.4 | async-start | bytes 8388608 | tf_op jit(solution)/shard_map/while
  96.3 5.2 %slice-start = ((s8[5013504]{0:T(1024)(128)(4,1)}), s8[4194304]{0:T(1024)(128)(4,1)S(1)}, s32[]{:S(2)}) async-start(s8[5013504]{0:T(1024)(128)(4,1)} %bitcast.191), calls=%async_computation.4 | async-start | bytes 8388608 | tf_op jit(solution)/shard_map/while
  107.8 5.2 %slice-start = ((s8[5013504]{0:T(1024)(128)(4,1)}), s8[4194304]{0:T(1024)(128)(4,1)S(1)}, s32[]{:S(2)}) async-start(s8[5013504]{0:T(1024)(128)(4,1)} %bitcast.191), calls=%async_computation.4 | async-start | bytes 8388608 | tf_op jit(solution)/shard_map/while
  119.2 5.2 %slice-start = ((s8[5013504]{0:T(1024)(128)(4,1)}), s8[4194304]{0:T(1024)(128)(4,1)S(1)}, s32[]{:S(2)}) async-start(s8[5013504]{0:T(1024)(128)(4,1)} %bitcast.191), calls=%async_computation.4 | async-start | bytes 8388608 | tf_op jit(solution)/shard_map/while
  119.3 5.2 %slice-start.1 = ((s8[5013504]{0:T(1024)(128)(4,1)}), s8[819200]{0:T(1024)(128)(4,1)S(1)}, s32[]{:S(2)}) async-start(s8[5013504]{0:T(1024)(128)(4,1)} %bitcast.191), calls=%async_computation.5 | async-start | bytes 1638400 | tf_op jit(solution)/shard_map/while
  130.7 5.2 %slice-start = ((s8[5013504]{0:T(1024)(128)(4,1)}), s8[4194304]{0:T(1024)(128)(4,1)S(1)}, s32[]{:S(2)}) async-start(s8[5013504]{0:T(1024)(128)(4,1)} %bitcast.191), calls=%async_computation.4 | async-start | bytes 8388608 | tf_op jit(solution)/shard_map/while
  142.2 5.2 %slice-start = ((s8[5013504]{0:T(1024)(128)(4,1)}), s8[4194304]{0:T(1024)(128)(4,1)S(1)}, s32[]{:S(2)}) async-start(s8[5013504]{0:T(1024)(128)(4,1)} %bitcast.191), calls=%async_computation.4 | async-start | bytes 8388608 | tf_op jit(solution)/shard_map/while
  159.8 7.7 %collective-permute-start.1 = (bf16[5,136,128]{2,1,0:T(8,128)(2,1)S(1)}, bf16[5,136,128]{2,1,0:T(8,128)(2,1)S(1)}, u32[]{:S(2)}, u32[]{:S(2)}) collective-permute-start(bf16[5,136,128]{2,1,0:T(8,128)(2,1)S(1)} %bitcast.207), channel_id=1, source_target_pairs={{16,0},{32,16},{48,32},{64,48},{80,64},{96,80},{112,96},{17,1},{33... | collective-permute-start | bytes 522248 | tf_op jit(solution)/shard_map/ppermute | solution.py:20
  161.1 7.2 %collective-permute-start = (bf16[5,136,128]{2,1,0:T(8,128)(2,1)S(1)}, bf16[5,136,128]{2,1,0:T(8,128)(2,1)S(1)}, u32[]{:S(2)}, u32[]{:S(2)}) collective-permute-start(bf16[5,136,128]{2,1,0:T(8,128)(2,1)S(1)} %bitcast.203), channel_id=1, source_target_pairs={{0,16},{16,32},{32,48},{48,64},{64,80},{80,96},{96,112},{1,17},{17... | collective-permute-start | bytes 522248 | tf_op jit(solution)/shard_map/ppermute | solution.py:18
  168.8 3.9 collective-permute-start.2
  170.8 6.2 %collective-permute-start.3 = (bf16[66,5,128]{2,1,0:T(8,128)(2,1)S(1)}, bf16[66,5,128]{2,1,0:T(8,128)(2,1)S(1)}, u32[]{:S(2)}, u32[]{:S(2)}) collective-permute-start(bf16[66,5,128]{2,1,0:T(8,128)(2,1)S(1)} %get-tuple-element.165), channel_id=1, source_target_pairs={{1,0},{2,1},{3,2},{4,3},{5,4},{6,5},{7,6},{8,7},{9,8},{10,9},{11,1... | collective-permute-start | bytes 253448 | tf_op jit(solution)/shard_map/ppermute | solution.py:20
  199.5 216.7 %all-reduce.5.cloned.1.call-start = ((), (), s32[]{:S(2)}) async-start(), calls=%async_computation.3 | async-start | bytes 1179648 | tf_op jit(solution)/shard_map/psum | solution.py:198
  (23 other events, 64.6 us)
Sparse Core Ops, SparseCore 0:
  199.6 73.7 all-reduce.2
  275.9 140.2 all-reduce.4
